TPU v7x, 32 devices: a whole 2x2x4 slice. The times are simulated.
32 devices in a mesh: dp: 16 (over z, y, x), tensor: 2 (over core).
Axes of the slice: x: 2, y: 2, z: 4, core: 2. Of those that a mesh axis runs over, the one named last changes fastest.
Arguments:
- inputs: bfloat16 [8192, 2048], P('dp'), may hold values from -6 to 6
- gamma_first: bfloat16 [2048], replicated, may hold values from 0.099609375 to 1.8984375
- beta_first: bfloat16 [2048], replicated, may hold values from -4 to 4
- heads_weight: bfloat16 [2048, 3, 2048], P('dp', None, 'tensor'), may hold values from -0.125 to 0.125
- output_weight: bfloat16 [2048, 2048], P('dp', 'tensor'), may hold values from -0.5 to 0.5
- output_bias: bfloat16 [2048], replicated, may hold values from -4 to 4
- gamma_second: bfloat16 [2048], replicated, may hold values from 0.099609375 to 1.8984375
- beta_second: bfloat16 [2048], replicated, may hold values from -4 to 4
- expand_weight: bfloat16 [2048, 8192], P('dp', 'tensor'), may hold values from -0.125 to 0.125
- expand_bias: bfloat16 [8192], P('tensor'), may hold values from -6 to 6
- reduce_weight: bfloat16 [2048, 8192], P('dp', 'tensor'), may hold values from -0.0625 to 0.0625
- reduce_bias: bfloat16 [2048], replicated, may hold values from -4 to 4
- group_sizes: int32 [32], P('dp'), may hold values from 4 to 16, as said below
- prefix_lengths: int32 [32], P('dp'), may hold values from 32 to 128, as said below
- solution_lengths: int32 [32, 16], P('dp'), may hold values from 1 to 221, as said below
- cotangent: bfloat16 [8192, 2048], P('dp'), may hold values from -6 to 6
Outputs:
- outputs: bfloat16 [8192, 2048], P('dp')
- input_gradient: bfloat16 [8192, 2048], P('dp')
- gamma_first_gradient: float32 [2048], P('dp')
- beta_first_gradient: float32 [2048], P('dp')
- heads_weight_gradient: float32 [2048, 3, 2048], P('dp', None, 'tensor')
- output_weight_gradient: float32 [2048, 2048], P('dp', 'tensor')
- output_bias_gradient: float32 [2048], P('dp')
- gamma_second_gradient: float32 [2048], P('dp')
- beta_second_gradient: float32 [2048], P('dp')
- expand_weight_gradient: float32 [2048, 8192], P('dp', 'tensor')
- expand_bias_gradient: float32 [2, 4096], P('tensor', 'dp')
- reduce_weight_gradient: float32 [2048, 8192], P('dp', 'tensor')
- reduce_bias_gradient: float32 [2048], P('dp')
Inputs may be any that keep to these rules, and one draw needn't show every extreme that they name: Each group has group_sizes solutions. `prefix_lengths`: A group's prefix and its first group_sizes solutions together take at most 256 token slots. `solution_lengths`: only a group's first group_sizes entries are used. The groups of a block fill at most 512 slots, and on at least one block exactly 512.
All inputs are finite; a program needn't handle non-finite values.
Results may differ from a plain program's by a relative error of at most 0.017.
Values may be sent and summed in bfloat16 or wider, within the bound.
No kernel may reach another device: no remote copies, remote signals or barrier semaphores. Data moves between devices by JAX's collectives and lax.ppermute only.
A program may use at most 384 MiB of HBM per device.

v0:
```python
import jax
import jax.numpy as jnp
from jax import lax
from jax.sharding import PartitionSpec as P

HEAD = 128


def layout(group_sizes, prefix_lengths, solution_lengths, row_count):
    entries = solution_lengths.shape[1]
    position = jnp.arange(entries, dtype=jnp.int32)
    counted = jnp.where(position[None, :] < group_sizes[:, None], solution_lengths, 0)
    pieces = jnp.concatenate([prefix_lengths[:, None], counted], axis=1).reshape(-1)
    bounds = jnp.cumsum(pieces)
    slot_index = jnp.arange(row_count, dtype=jnp.int32)
    piece_index = jnp.sum((slot_index[:, None] >= bounds[None, :]).astype(jnp.int32), axis=1)
    live_rows = piece_index < pieces.shape[0]
    group_index = piece_index // (entries + 1)
    opening = piece_index % (entries + 1) == 0
    same_group = (
        (group_index[:, None] == group_index[None, :]) & live_rows[:, None] & live_rows[None, :]
    )
    causal = slot_index[None, :] <= slot_index[:, None]
    visible = opening[None, :] | (piece_index[:, None] == piece_index[None, :])
    allowed = (slot_index[:, None] == slot_index[None, :]) | same_group & causal & visible
    return (allowed, live_rows)


def normalize(values, gain_vector, shift_vector):
    center = values - jnp.mean(values, axis=-1, keepdims=True)
    spread = jnp.mean(center * center, axis=-1, keepdims=True)
    return center * lax.rsqrt(spread + 1e-05) * gain_vector + shift_vector


def smooth(values):
    return jax.nn.gelu(values, approximate=True)


def body(
    inputs,
    gamma_first,
    beta_first,
    heads_weight,
    output_weight,
    output_bias,
    gamma_second,
    beta_second,
    expand_weight,
    expand_bias,
    reduce_weight,
    reduce_bias,
    group_sizes,
    prefix_lengths,
    solution_lengths,
    cotangent,
):
    row_count = inputs.shape[0]
    local_width = output_weight.shape[1]
    local_heads = local_width // HEAD
    score_scale = HEAD ** (-0.5)
    across = (((1,), (1,)), ((), ()))
    token_dims = (((0,), (0,)), ((), ()))
    allowed, live_rows = layout(group_sizes, prefix_lengths, solution_lengths, row_count)
    live_mask = live_rows.astype(jnp.float32)[:, None]
    gain_first = gamma_first.astype(jnp.float32)
    shift_first = beta_first.astype(jnp.float32)
    gain_second = gamma_second.astype(jnp.float32)
    shift_second = beta_second.astype(jnp.float32)
    residual = inputs.astype(jnp.float32)
    first_low = normalize(residual, gain_first, shift_first).astype(jnp.bfloat16)
    heads_full, output_full = (
        lax.all_gather(heads_weight, "dp", axis=0, tiled=True),
        lax.all_gather(output_weight, "dp", axis=0, tiled=True),
    )
    projected = jnp.einsum(
        "td,dch->tch", first_low, heads_full, preferred_element_type=jnp.float32
    ).astype(jnp.bfloat16)
    queries = projected[:, 0].reshape(row_count, local_heads, HEAD)
    keyset = projected[:, 1].reshape(row_count, local_heads, HEAD)
    valueset = projected[:, 2].reshape(row_count, local_heads, HEAD)

    def masked_scores():
        raw_scores = (
            jnp.einsum("qhe,khe->hqk", queries, keyset, preferred_element_type=jnp.float32)
            * score_scale
        )
        return jnp.where(allowed[None], raw_scores, -1e30)

    scores = masked_scores()
    row_peak = jnp.max(scores, axis=-1, keepdims=True)
    exponent = jnp.exp(scores - row_peak)
    row_total = jnp.sum(exponent, axis=-1, keepdims=True)
    soft_weights = exponent / row_total
    log_total = row_peak + jnp.log(row_total)
    soft_low = soft_weights.astype(jnp.bfloat16)
    mixed_heads = (
        jnp.einsum("hqk,khe->qhe", soft_low, valueset, preferred_element_type=jnp.float32)
        .reshape(row_count, local_width)
        .astype(jnp.bfloat16)
    )
    attended = lax.psum(
        lax.dot_general(mixed_heads, output_full, across, preferred_element_type=jnp.float32),
        "tensor",
    )
    middle = residual + attended + output_bias.astype(jnp.float32)
    second_low = normalize(middle, gain_second, shift_second).astype(jnp.bfloat16)
    columns = second_low
    hidden_sum = jnp.dot(
        columns,
        lax.all_gather(expand_weight, "dp", axis=0, tiled=True),
        preferred_element_type=jnp.float32,
    ) + expand_bias.astype(jnp.float32)
    hidden_low = smooth(hidden_sum).astype(jnp.bfloat16)
    branch = lax.psum(
        lax.dot_general(
            hidden_low,
            lax.all_gather(reduce_weight, "dp", axis=0, tiled=True),
            across,
            preferred_element_type=jnp.float32,
        ).astype(jnp.bfloat16),
        "tensor",
    ).astype(jnp.float32)
    outputs = (live_mask * (middle + branch + reduce_bias.astype(jnp.float32))).astype(jnp.bfloat16)
    upstream = live_mask * cotangent.astype(jnp.float32)
    reduce_bias_gradient = jnp.sum(upstream, axis=0)
    upstream_low = upstream.astype(jnp.bfloat16)
    columns = upstream_low
    hidden_tangent = jnp.dot(
        columns,
        lax.all_gather(reduce_weight, "dp", axis=0, tiled=True),
        preferred_element_type=jnp.float32,
    )
    _, smooth_pullback = jax.vjp(smooth, hidden_sum)
    sum_tangent = smooth_pullback(hidden_tangent)[0]
    expand_bias_gradient = jnp.sum(sum_tangent, axis=0)[None, :]
    sum_low = sum_tangent.astype(jnp.bfloat16)
    second_tangent = lax.psum(
        lax.dot_general(
            sum_low,
            lax.all_gather(expand_weight, "dp", axis=0, tiled=True),
            across,
            preferred_element_type=jnp.float32,
        ).astype(jnp.bfloat16),
        "tensor",
    ).astype(jnp.float32)
    feed_totals = lax.psum_scatter(
        jnp.stack(
            [
                lax.dot_general(
                    second_low, sum_low, token_dims, preferred_element_type=jnp.float32
                ),
                lax.dot_general(
                    upstream_low, hidden_low, token_dims, preferred_element_type=jnp.float32
                ),
            ],
            axis=1,
        ),
        "dp",
        scatter_dimension=0,
        tiled=True,
    )
    expand_share = feed_totals[:, 0]
    reduce_share = feed_totals[:, 1]
    _, second_pullback = jax.vjp(normalize, middle, gain_second, shift_second)
    middle_part, gamma_second_gradient, beta_second_gradient = second_pullback(second_tangent)
    middle_tangent = upstream + middle_part
    output_bias_gradient = jnp.sum(middle_tangent, axis=0)
    middle_low = middle_tangent.astype(jnp.bfloat16)
    mixed_tangent = (
        jnp.dot(middle_low, output_full, preferred_element_type=jnp.float32)
        .astype(jnp.bfloat16)
        .reshape(row_count, local_heads, HEAD)
    )
    soft_again = jnp.exp(masked_scores() - log_total)
    soft_again_low = soft_again.astype(jnp.bfloat16)
    value_tangent = jnp.einsum(
        "hqk,qhe->khe", soft_again_low, mixed_tangent, preferred_element_type=jnp.float32
    )
    weight_tangent = jnp.einsum(
        "qhe,khe->hqk", mixed_tangent, valueset, preferred_element_type=jnp.float32
    )
    score_tangent = (
        soft_again * (weight_tangent - jnp.sum(soft_again * weight_tangent, axis=-1, keepdims=True))
    ).astype(jnp.bfloat16)
    query_tangent = (
        jnp.einsum("hqk,khe->qhe", score_tangent, keyset, preferred_element_type=jnp.float32)
        * score_scale
    )
    key_tangent = (
        jnp.einsum("hqk,qhe->khe", score_tangent, queries, preferred_element_type=jnp.float32)
        * score_scale
    )
    projected_tangent = (
        jnp.stack([query_tangent, key_tangent, value_tangent], axis=1)
        .reshape(row_count, 3, local_width)
        .astype(jnp.bfloat16)
    )
    first_tangent = lax.psum(
        jnp.einsum(
            "tch,dch->td", projected_tangent, heads_full, preferred_element_type=jnp.float32
        ).astype(jnp.bfloat16),
        "tensor",
    ).astype(jnp.float32)
    heads_term = jnp.einsum(
        "tc,tkh->ckh", first_low, projected_tangent, preferred_element_type=jnp.float32
    )
    output_term = lax.dot_general(
        middle_low, mixed_heads, token_dims, preferred_element_type=jnp.float32
    )
    head_totals = lax.psum_scatter(
        jnp.concatenate([heads_term, output_term[:, None, :]], axis=1),
        "dp",
        scatter_dimension=0,
        tiled=True,
    )
    _, first_pullback = jax.vjp(normalize, residual, gain_first, shift_first)
    input_part, gamma_first_gradient, beta_first_gradient = first_pullback(first_tangent)
    input_gradient = (middle_tangent + input_part).astype(jnp.bfloat16)
    vectors = (
        lax.psum_scatter(gamma_first_gradient, "dp", scatter_dimension=0, tiled=True),
        lax.psum_scatter(beta_first_gradient, "dp", scatter_dimension=0, tiled=True),
        lax.psum_scatter(output_bias_gradient, "dp", scatter_dimension=0, tiled=True),
        lax.psum_scatter(gamma_second_gradient, "dp", scatter_dimension=0, tiled=True),
        lax.psum_scatter(beta_second_gradient, "dp", scatter_dimension=0, tiled=True),
        lax.psum_scatter(reduce_bias_gradient, "dp", scatter_dimension=0, tiled=True),
        lax.psum_scatter(expand_bias_gradient, "dp", scatter_dimension=1, tiled=True),
    )
    return (
        outputs,
        input_gradient,
        vectors[0],
        vectors[1],
        head_totals[:, :3],
        head_totals[:, 3],
        vectors[2],
        vectors[3],
        vectors[4],
        expand_share,
        vectors[6],
        reduce_share,
        vectors[5],
    )


def solution(mesh):
    placed = (
        P("dp", None),
        P(),
        P(),
        P("dp", None, "tensor"),
        P("dp", "tensor"),
        P(),
        P(),
        P(),
        P("dp", "tensor"),
        P("tensor"),
        P("dp", "tensor"),
        P(),
        P("dp"),
        P("dp"),
        P("dp", None),
        P("dp", None),
    )
    return jax.shard_map(
        body,
        mesh=mesh,
        in_specs=placed,
        out_specs=(
            P("dp", None),
            P("dp", None),
            P("dp"),
            P("dp"),
            P("dp", None, "tensor"),
            P("dp", "tensor"),
            P("dp"),
            P("dp"),
            P("dp"),
            P("dp", "tensor"),
            P("tensor", "dp"),
            P("dp", "tensor"),
            P("dp"),
        ),
        check_vma=False,
    )
```

profile of v0, /device:TPU:10, one launch (start us, length us, event | category | flops | bytes accessed | tf_op | source)
XLA Modules:
  0.0 2903.4 jit_solution(15388383072456782599)
XLA Ops:
  16.1 145.8 %all-gather.5.cloned.1.call-done = bf16[2048,3,1024]{2,0,1:T(8,128)(2,1)} async-done(((bf16[128,3,1024]{2,0,1:T(8,128)(2,1)}), bf16[2048,3,1024]{2,0,1:T(8,128)(2,1)}) %all-gather.5.cloned.1.call-update) | async-done | bytes 12582928 | tf_op jit(solution)/shard_map/all_gather | solution.py:72
  162.0 9.7 convolution_convert_fusion.2
  178.9 2.9 fusion.66
  187.9 53.0 %all-gather.7.cloned.1.call-done = bf16[2048,1024]{1,0:T(8,128)(2,1)} async-done(((bf16[128,1024]{1,0:T(8,128)(2,1)}), bf16[2048,1024]{1,0:T(8,128)(2,1)}) %all-gather.7.cloned.1.call-update) | async-done | bytes 4194320 | tf_op jit(solution)/shard_map/all_gather | solution.py:73
  240.9 6.8 fusion.68
  249.2 26.0 all-reduce.12.cloned.1.call-done
  275.2 2.8 fusion.64
  280.6 188.2 %all-gather.9.cloned.1.call-done = bf16[2048,4096]{1,0:T(8,128)(2,1)} async-done(((bf16[128,4096]{1,0:T(8,128)(2,1)}), bf16[2048,4096]{1,0:T(8,128)(2,1)}) %all-gather.9.cloned.1.call-update) | async-done | bytes 16777232 | tf_op jit(solution)/shard_map/all_gather | solution.py:110
  468.9 15.8 fusion.61
  484.7 177.0 %all-gather.11.cloned.1.call-done = bf16[2048,4096]{1,0:T(8,128)(2,1)} async-done(((bf16[128,4096]{1,0:T(8,128)(2,1)}), bf16[2048,4096]{1,0:T(8,128)(2,1)}) %all-gather.11.cloned.1.call-update) | async-done | bytes 16777232 | tf_op jit(solution)/shard_map/all_gather | solution.py:117
  661.7 18.5 fusion.67
  682.2 13.4 convolution_convert_fusion
  697.7 18.8 convolution_convert_fusion.1
  717.3 4.6 convert_reduce_fusion.1
  724.6 2.8 fusion.62
  732.3 5.1 fusion.35
  737.4 4.8 multiply_reduce_fusion
  750.3 11.3 bitcast_convert_fusion
  761.8 5.1 convolution_bitcast_fusion.2
  767.0 12.0 fusion.38
  779.0 20.2 pad_maximum_fusion.1
  799.9 20.1 convolution_bitcast_fusion.1
  820.1 19.7 convolution_bitcast_fusion
  839.8 44.5 %pad_maximum_fusion = f32[2048,2,4096]{2,0,1:T(8,128)} fusion(f32[2048,1,4096]{2,0,1:T(8,128)} %convolution_bitcast_fusion, f32[2048,1,4096]{2,0,1:T(8,128)} %convolution_bitcast_fusion.1), kind=kLoop, calls=%fused_computation | loop fusion | flops 16777216 | bytes 134217728 | tf_op jit(solution)/shard_map/stack | solution.py:147
  887.8 2.9 convert_reduce_fusion
  893.3 71.1 %all-reduce.6 = (f32[2048]{0:T(1024)S(1)}, f32[2048]{0:T(1024)S(1)}, f32[2048]{0:T(1024)S(1)}, f32[2048]{0:T(1024)S(1)}, f32[2048]{0:T(1024)S(1)}, /*index=5*/f32[2048]{0:T(1024)S(1)}) all-reduce(f32[2048]{0:T(1024)S(1)} %get-tuple-element.15, f32[2048]{0:T(1024)S(1)} %get-tuple-element.19, ...), channel_id=2, replica_groups=mesh['dp'=16,'tensor'=2] {'dp'}, use_global_device_ids=true, to_apply=%region_18.19.clone | all-reduce | flops 12288 | bytes 98304
  967.8 4.9 multiply_convert_fusion.2
  972.9 2.8 add_convert_fusion
  975.7 550.2 %reduce-scatter.6.cloned.1.call-done = f32[128,4,1024]{2,0,1:T(8,128)} async-done(((f32[2048,4,1024]{2,0,1:T(8,128)}), f32[128,4,1024]{2,0,1:T(8,128)}) %reduce-scatter.6.cloned.1.call-update) | async-done | bytes 2097168 | tf_op jit(solution)/shard_map/reduce_scatter | solution.py:210
  1525.9 2.7 slice.31
  1530.5 1360.9 %reduce-scatter.8.cloned.1.call-done = f32[128,2,4096]{2,0,1:T(8,128)} async-done(((f32[2048,2,4096]{2,0,1:T(8,128)}), f32[128,2,4096]{2,0,1:T(8,128)}) %reduce-scatter.8.cloned.1.call-update) | async-done | bytes 4194320 | tf_op jit(solution)/shard_map/reduce_scatter | solution.py:146
  2891.4 4.7 slice_bitcast_fusion
  (173 shorter events, 57.9 us)
Async XLA Ops:
  7.2 6.8 copy-start.3
  7.2 154.8 %all-gather.5.cloned.1.call-start = ((), (), s32[]{:S(2)}) async-start(), calls=%async_computation.3 | async-start | bytes 13369344 | tf_op jit(solution)/shard_map/all_gather | solution.py:72
  7.9 232.9 %all-gather.7.cloned.1.call-start = ((), (), s32[]{:S(2)}) async-start(), calls=%async_computation.4 | async-start | bytes 4456448 | tf_op jit(solution)/shard_map/all_gather | solution.py:73
  8.7 266.5 %all-reduce.12.cloned.1.call-start = ((), (), s32[]{:S(2)}) async-start(), calls=%async_computation.5 | async-start | bytes 8388608 | tf_op jit(solution)/shard_map/psum | solution.py:101
  10.2 161.6 %copy-start.21 = (f32[2048]{0:T(1024)}, f32[2048]{0:T(1024)S(1)}, u32[]{:S(2)}) copy-start(f32[2048]{0:T(1024)S(1)} %convert_element_type.107) | copy-start | bytes 24580
  10.8 160.9 %copy-start.34 = (f32[2048]{0:T(1024)}, f32[2048]{0:T(1024)S(1)}, u32[]{:S(2)}) copy-start(f32[2048]{0:T(1024)S(1)} %convert_element_type.108) | copy-start | bytes 24580
  14.0 157.7 %copy-start.23 = (f32[512]{0:T(512)}, f32[512]{0:T(512)S(1)}, u32[]{:S(2)}) copy-start(f32[512]{0:T(512)S(1)} %broadcast_multiply_fusion.1) | copy-start | bytes 6148
  14.7 157.0 %copy-start.29 = (f32[512]{0:T(512)}, f32[512]{0:T(512)S(1)}, u32[]{:S(2)}) copy-start(f32[512]{0:T(512)S(1)} %fusion.56) | copy-start | bytes 6148
  176.2 5.6 copy-start.10
  247.7 221.2 %all-gather.9.cloned.1.call-start = ((), (), s32[]{:S(2)}) async-start(), calls=%async_computation.6 | async-start | bytes 17825792 | tf_op jit(solution)/shard_map/all_gather | solution.py:110
  248.3 413.4 %all-gather.11.cloned.1.call-start = ((), (), s32[]{:S(2)}) async-start(), calls=%async_computation.7 | async-start | bytes 17825792 | tf_op jit(solution)/shard_map/all_gather | solution.py:117
  248.9 468.4 %all-reduce.14.cloned.1.call-start = ((), (), s32[]{:S(2)}) async-start(), calls=%async_computation.8 | async-start | bytes 4194304 | tf_op jit(solution)/shard_map/psum | solution.py:137
  249.2 219.7 %copy-start.36 = (f32[2048]{0:T(1024)}, f32[2048]{0:T(1024)S(1)}, u32[]{:S(2)}) copy-start(f32[2048]{0:T(1024)S(1)} %convert_element_type.117) | copy-start | bytes 24580
  280.6 381.1 %copy-start.14 = (bf16[512,2048]{1,0:T(8,128)(2,1)S(1)}, bf16[512,2048]{1,0:T(8,128)(2,1)}, u32[]{:S(2)}) copy-start(bf16[512,2048]{1,0:T(8,128)(2,1)} %param.31) | copy-start | bytes 6291460
  695.6 190.6 %reduce-scatter.10.cloned.1.call-start = ((), (), s32[]{:S(2)}) async-start(), calls=%async_computation.11 | async-start | bytes 2228224
  697.7 190.1 %all-reduce.16.cloned.1.call-start = ((), (), s32[]{:S(2)}) async-start(), calls=%async_computation.12 | async-start | bytes 8388608 | tf_op jit(solution)/shard_map/psum | solution.py:114
  732.3 9.9 slice-start
  750.3 11.4 copy-start.19
  761.7 5.2 copy-start.4
  761.7 5.2 copy-start.17
  761.7 5.2 copy-start.22
  761.7 5.2 copy-start.24
  761.7 5.2 copy-start.30
  761.7 5.2 copy-start.35
  761.8 764.1 %reduce-scatter.6.cloned.1.call-start = ((), (), s32[]{:S(2)}) async-start(), calls=%async_computation.9 | async-start | bytes 35651584 | tf_op jit(solution)/shard_map/reduce_scatter | solution.py:210
  799.3 2092.1 %reduce-scatter.8.cloned.1.call-start = ((), (), s32[]{:S(2)}) async-start(), calls=%async_computation.10 | async-start | bytes 71303168 | tf_op jit(solution)/shard_map/reduce_scatter | solution.py:146
  799.9 20.1 copy-start.15
  884.3 6.4 copy-start.32
  887.8 5.4 copy-start.25
  887.8 5.4 copy-start.26
  887.8 5.4 copy-start.27
  887.8 5.4 copy-start.28
  (25 other events, 69.6 us)
Sparse Core Ops, SparseCore 0:
  10.8 151.1 all-gather.4
  164.7 76.1 all-gather.6
  247.8 27.2 all-reduce.11
  278.2 190.6 all-gather.8
  471.9 189.7 all-gather.10
  695.7 21.5 all-reduce.13
  720.2 71.8 reduce-scatter.9
  795.2 35.4 all-reduce.15
  833.2 692.6 reduce-scatter.5
  1528.2 1363.1 reduce-scatter.7
where the time goes:
time: 2910 us; the launch traced here: 2900 us
  waiting for transfers between devices  2500 us (86%)
  matrix products  171 us (6%)
  other arithmetic  101 us (3%)
  blocking collectives  71.1 us (2%)
  local copies, waits for them, and re-layouts  38.9 us (1%)
    reduce_scatter x1, waiting for transfers between devices, body(): lax.psum_scatter(jnp.stack([lax.dot_general(second_low, sum_low, token_di...  1360 us
    reduce_scatter x1, waiting for transfers between devices, body(): lax.psum_scatter(jnp.concatenate([heads_term, output_term[:, None, :]], a...  550 us
    all_gather x1, waiting for transfers between devices, body(): lax.all_gather(expand_weight, 'dp', axis=0, tiled=True)  188 us
    all_gather x1, waiting for transfers between devices, body(): lax.all_gather(reduce_weight, 'dp', axis=0, tiled=True)  177 us
    all_gather x1, waiting for transfers between devices, body(): lax.all_gather(heads_weight, 'dp', axis=0, tiled=True)  146 us
    unnamed x1, blocking collectives  71.1 us
  transfers between devices with their start and end apart: 10, of which 8 were waited for; matrix products, arithmetic and copies ran while one was open for 9% of the time, Pallas kernels for 0%

commit v1 on v0

--- a/solution.py
+++ b/solution.py
@@ -4,6 +4,18 @@
 from jax.sharding import PartitionSpec as P
 
 HEAD = 128
+
+
+def ring_gather(array, axis, dim):
+    ways, here, lap = (lax.axis_size(axis), lax.axis_index(axis), array.shape[dim])
+    dims = [n * ways if d == dim else n for d, n in enumerate(array.shape)]
+    full = lax.dynamic_update_slice_in_dim(
+        jnp.zeros(dims, array.dtype), array, here * lap, axis=dim
+    )
+    for far in range(1, ways):
+        array = lax.ppermute(array, axis, [(d, (d + 1) % ways) for d in range(ways)])
+        full = lax.dynamic_update_slice_in_dim(full, array, (here - far) % ways * lap, axis=dim)
+    return full
 
 
 def layout(group_sizes, prefix_lengths, solution_lengths, row_count):
@@ -69,7 +81,7 @@
     residual = inputs.astype(jnp.float32)
     first_low = normalize(residual, gain_first, shift_first).astype(jnp.bfloat16)
     heads_full, output_full = (
-        lax.all_gather(heads_weight, "dp", axis=0, tiled=True),
+        ring_gather(heads_weight, "dp", 0),
         lax.all_gather(output_weight, "dp", axis=0, tiled=True),
     )
     projected = jnp.einsum(

time: 2910 us -> 3030 us (1.041)
  waiting for transfers between devices: 2500 us -> 2560 us
  starting transfers between devices: 0.58 us -> 36.1 us
  local copies, waits for them, and re-layouts: 38.9 us -> 69.9 us
    ppermute x0 -> x15, waiting for transfers between devices: none -> 230 us  [ring_gather(): lax.ppermute(array, axis, [(d, (d + 1) % ways) for d in range(ways)])]
    all_gather x1 -> x0, waiting for transfers between devices: 146 us -> none  [body(): lax.all_gather(heads_weight, 'dp', axis=0, tiled=True)]
    all_gather x1, waiting for transfers between devices: 53 us -> 0.01 us  [body(): lax.all_gather(output_weight, 'dp', axis=0, tiled=True)]
    ppermute x0 -> x15, starting transfers between devices: none -> 35.6 us  [ring_gather(): lax.ppermute(array, axis, [(d, (d + 1) % ways) for d in range(ways)])]
  transfers between devices with their start and end apart: 10 -> 24, of which waited for: 8 -> 21; matrix products, arithmetic and copies ran while one was open for 9% -> 9% of each run, Pallas kernels for 0% -> 0%
where the time goes in v1:
time: 3030 us
  waiting for transfers between devices  2560 us (84%)
  matrix products  173 us (6%)
  other arithmetic  101 us (3%)
  local copies, waits for them, and re-layouts  69.9 us (2%)
  blocking collectives  69.5 us (2%)
  starting transfers between devices  36.1 us (1%)
    reduce_scatter x1, waiting for transfers between devices, body(): lax.psum_scatter(jnp.stack([lax.dot_general(second_low, sum_low, token_di...  1360 us
    reduce_scatter x1, waiting for transfers between devices, body(): lax.psum_scatter(jnp.concatenate([heads_term, output_term[:, None, :]], a...  549 us
    ppermute x15, waiting for transfers between devices, ring_gather(): lax.ppermute(array, axis, [(d, (d + 1) % ways) for d in range(ways)])  230 us
    all_gather x1, waiting for transfers between devices, body(): lax.all_gather(expand_weight, 'dp', axis=0, tiled=True)  188 us
    all_gather x1, waiting for transfers between devices, body(): lax.all_gather(reduce_weight, 'dp', axis=0, tiled=True)  177 us
    unnamed x1, blocking collectives  69.5 us
  transfers between devices with their start and end apart: 24, of which 21 were waited for; matrix products, arithmetic and copies ran while one was open for 9% of the time, Pallas kernels for 0%

profile of v1, /device:TPU:10, one launch (start us, length us, event | category | flops | bytes accessed | tf_op | source)
XLA Modules:
  0.0 3025.1 jit_solution(2730310762770265056)
XLA Ops:
  8.8 18.0 collective-permute-done
  29.2 16.6 collective-permute-done.1
  48.5 16.6 collective-permute-done.2
  66.9 16.6 collective-permute-done.3
  84.6 16.3 collective-permute-done.4
  102.1 16.5 collective-permute-done.5
  119.5 16.8 collective-permute-done.6
  137.2 15.2 collective-permute-done.7
  153.8 17.0 collective-permute-done.8
  171.5 17.0 collective-permute-done.9
  194.7 13.4 collective-permute-done.10
  212.7 19.9 collective-permute-done.11
  232.6 8.2 collective-permute-start.12
  255.3 7.8 collective-permute-start.13
  268.8 23.5 collective-permute-done.13
  310.8 9.8 convolution_convert_fusion.2
  345.3 51.9 %all-reduce.12.cloned.1.call-done = f32[512,2048]{1,0:T(8,128)} async-done(((f32[512,2048]{1,0:T(8,128)}), f32[512,2048]{1,0:T(8,128)}) %all-reduce.12.cloned.1.call-update) | async-done | bytes 4194320 | tf_op jit(solution)/shard_map/psum | solution.py:113
  402.6 188.4 %all-gather.6.cloned.1.call-done = bf16[2048,4096]{1,0:T(8,128)(2,1)} async-done(((bf16[128,4096]{1,0:T(8,128)(2,1)}), bf16[2048,4096]{1,0:T(8,128)(2,1)}) %all-gather.6.cloned.1.call-update) | async-done | bytes 16777232 | tf_op jit(solution)/shard_map/all_gather | solution.py:122
  591.0 15.8 fusion.61
  606.8 177.1 %all-gather.8.cloned.1.call-done = bf16[2048,4096]{1,0:T(8,128)(2,1)} async-done(((bf16[128,4096]{1,0:T(8,128)(2,1)}), bf16[2048,4096]{1,0:T(8,128)(2,1)}) %all-gather.8.cloned.1.call-update) | async-done | bytes 16777232 | tf_op jit(solution)/shard_map/all_gather | solution.py:129
  783.9 18.5 fusion.67
  804.4 13.4 convolution_convert_fusion
  819.9 18.8 convolution_convert_fusion.1
  875.1 11.0 bitcast_convert_fusion
  891.4 12.2 fusion.38
  903.5 20.3 pad_maximum_fusion.1
  924.5 20.1 convolution_bitcast_fusion.1
  944.6 20.2 convolution_bitcast_fusion
  964.8 44.5 %pad_maximum_fusion = f32[2048,2,4096]{2,0,1:T(8,128)} fusion(f32[2048,1,4096]{2,0,1:T(8,128)} %convolution_bitcast_fusion, f32[2048,1,4096]{2,0,1:T(8,128)} %convolution_bitcast_fusion.1), kind=kLoop, calls=%fused_computation | loop fusion | flops 16777216 | bytes 134217728 | tf_op jit(solution)/shard_map/stack | solution.py:159
  1018.3 69.5 %all-reduce.6 = (f32[2048]{0:T(1024)S(1)}, f32[2048]{0:T(1024)S(1)}, f32[2048]{0:T(1024)S(1)}, f32[2048]{0:T(1024)S(1)}, f32[2048]{0:T(1024)S(1)}, /*index=5*/f32[2048]{0:T(1024)S(1)}) all-reduce(f32[2048]{0:T(1024)S(1)} %get-tuple-element.15, f32[2048]{0:T(1024)S(1)} %get-tuple-element.19, ...), channel_id=2, replica_groups=mesh['dp'=16,'tensor'=2] {'dp'}, use_global_device_ids=true, to_apply=%region_18.19.clone | all-reduce | flops 12288 | bytes 98304
  1099.2 548.7 %reduce-scatter.6.cloned.1.call-done = f32[128,4,1024]{2,0,1:T(8,128)} async-done(((f32[2048,4,1024]{2,0,1:T(8,128)}), f32[128,4,1024]{2,0,1:T(8,128)}) %reduce-scatter.6.cloned.1.call-update) | async-done | bytes 2097168 | tf_op jit(solution)/shard_map/reduce_scatter | solution.py:222
  1652.6 1361.1 %reduce-scatter.8.cloned.1.call-done = f32[128,2,4096]{2,0,1:T(8,128)} async-done(((f32[2048,2,4096]{2,0,1:T(8,128)}), f32[128,2,4096]{2,0,1:T(8,128)}) %reduce-scatter.8.cloned.1.call-update) | async-done | bytes 4194320 | tf_op jit(solution)/shard_map/reduce_scatter | solution.py:158
  (251 shorter events, 168.8 us)
Async XLA Ops:
  7.2 204.1 %copy-start.3 = (bf16[512,2048]{1,0:T(8,128)(2,1)S(1)}, bf16[512,2048]{1,0:T(8,128)(2,1)}, u32[]{:S(2)}) copy-start(bf16[512,2048]{1,0:T(8,128)(2,1)} %param.16) | copy-start | bytes 6291460
  7.2 329.5 %all-gather.4.cloned.1.call-start = ((), (), s32[]{:S(2)}) async-start(), calls=%async_computation.3 | async-start | bytes 4456448 | tf_op jit(solution)/shard_map/all_gather | solution.py:85
  7.2 19.5 collective-permute-start
  26.8 56.7 %copy-start.24 = (bf16[128,3,1024]{2,0,1:T(8,128)(2,1)}, bf16[128,3,1024]{2,0,1:T(8,128)(2,1)S(1)}, u32[]{:S(2)}) copy-start(bf16[128,3,1024]{2,0,1:T(8,128)(2,1)S(1)} %collective-permute-done) | copy-start | bytes 2359300
  26.8 19.0 collective-permute-start.1
  45.8 19.3 collective-permute-start.2
  65.1 18.4 collective-permute-start.3
  83.4 17.4 collective-permute-start.4
  101.8 16.8 collective-permute-start.5
  119.5 16.8 collective-permute-start.6
  137.2 15.2 collective-permute-start.7
  153.3 17.5 collective-permute-start.8
  170.8 17.7 collective-permute-start.9
  171.4 225.7 %all-reduce.12.cloned.1.call-start = ((), (), s32[]{:S(2)}) async-start(), calls=%async_computation.4 | async-start | bytes 8388608 | tf_op jit(solution)/shard_map/psum | solution.py:113
  188.5 19.6 collective-permute-start.10
  190.8 120.0 %copy-start.38 = (f32[2048]{0:T(1024)}, f32[2048]{0:T(1024)S(1)}, u32[]{:S(2)}) copy-start(f32[2048]{0:T(1024)S(1)} %convert_element_type.107) | copy-start | bytes 24580
  191.5 119.3 %copy-start.51 = (f32[2048]{0:T(1024)}, f32[2048]{0:T(1024)S(1)}, u32[]{:S(2)}) copy-start(f32[2048]{0:T(1024)S(1)} %convert_element_type.108) | copy-start | bytes 24580
  194.7 116.1 %copy-start.40 = (f32[512]{0:T(512)}, f32[512]{0:T(512)S(1)}, u32[]{:S(2)}) copy-start(f32[512]{0:T(512)S(1)} %broadcast_multiply_fusion.1) | copy-start | bytes 6148
  208.1 24.5 collective-permute-start.11
  212.6 98.2 %copy-start.46 = (f32[512]{0:T(512)}, f32[512]{0:T(512)S(1)}, u32[]{:S(2)}) copy-start(f32[512]{0:T(512)S(1)} %fusion.56) | copy-start | bytes 6148
  232.6 22.7 collective-permute-start.12
  255.3 37.0 %collective-permute-start.13 = (bf16[128,3,1024]{2,0,1:T(8,128)(2,1)}, bf16[128,3,1024]{2,0,1:T(8,128)(2,1)S(1)}, u32[]{:S(2)}, u32[]{:S(2)}) collective-permute-start(bf16[128,3,1024]{2,0,1:T(8,128)(2,1)} %collective-permute-done.12), channel_id=1, source_target_pairs={{0,2},{2,4},{4,6},{6,8},{8,10},{10,12},{12,14},{14,16},{16,18},{18... | collective-permute-start | bytes 2359304 | tf_op jit(solution)/shard_map/ppermute | solution.py:16
  292.3 17.6 collective-permute-start.14
  343.6 247.4 %all-gather.6.cloned.1.call-start = ((), (), s32[]{:S(2)}) async-start(), calls=%async_computation.5 | async-start | bytes 17825792 | tf_op jit(solution)/shard_map/all_gather | solution.py:122
  344.4 439.5 %all-gather.8.cloned.1.call-start = ((), (), s32[]{:S(2)}) async-start(), calls=%async_computation.6 | async-start | bytes 17825792 | tf_op jit(solution)/shard_map/all_gather | solution.py:129
  345.0 494.5 %all-reduce.14.cloned.1.call-start = ((), (), s32[]{:S(2)}) async-start(), calls=%async_computation.7 | async-start | bytes 4194304 | tf_op jit(solution)/shard_map/psum | solution.py:149
  345.2 245.8 %copy-start.53 = (f32[2048]{0:T(1024)}, f32[2048]{0:T(1024)S(1)}, u32[]{:S(2)}) copy-start(f32[2048]{0:T(1024)S(1)} %convert_element_type.117) | copy-start | bytes 24580
  402.6 381.3 %copy-start.15 = (bf16[512,2048]{1,0:T(8,128)(2,1)S(1)}, bf16[512,2048]{1,0:T(8,128)(2,1)}, u32[]{:S(2)}) copy-start(bf16[512,2048]{1,0:T(8,128)(2,1)} %param.31) | copy-start | bytes 6291460
  817.8 193.5 %reduce-scatter.10.cloned.1.call-start = ((), (), s32[]{:S(2)}) async-start(), calls=%async_computation.10 | async-start | bytes 2228224
  819.9 193.0 %all-reduce.16.cloned.1.call-start = ((), (), s32[]{:S(2)}) async-start(), calls=%async_computation.11 | async-start | bytes 8388608 | tf_op jit(solution)/shard_map/psum | solution.py:126
  886.2 761.8 %reduce-scatter.6.cloned.1.call-start = ((), (), s32[]{:S(2)}) async-start(), calls=%async_computation.8 | async-start | bytes 35651584 | tf_op jit(solution)/shard_map/reduce_scatter | solution.py:222
  923.8 2089.8 %reduce-scatter.8.cloned.1.call-start = ((), (), s32[]{:S(2)}) async-start(), calls=%async_computation.9 | async-start | bytes 71303168 | tf_op jit(solution)/shard_map/reduce_scatter | solution.py:158
  (56 other events, 398.1 us)
Sparse Core Ops, SparseCore 0:
  171.6 132.7 all-gather.3
  343.8 53.3 all-reduce.11
  400.3 190.6 all-gather.5
  594.0 189.7 all-gather.7
  817.9 21.5 all-reduce.13
  842.2 72.1 reduce-scatter.9
  917.4 35.3 all-reduce.15
  955.3 692.5 reduce-scatter.5
  1650.4 1363.1 reduce-scatter.7
